TPU v7x, 32 devices: a whole 2x2x4 slice. The times are simulated.
32 devices in a mesh: dp: 16 (over z, y, core), pipe: 2 (over x).
Axes of the slice: x: 2, y: 2, z: 4, core: 2. Of those that a mesh axis runs over, the one named last changes fastest.
Arguments:
- clean: bfloat16 [64, 128, 320], P('dp'), may hold values from -20 to 20
- noise: bfloat16 [64, 128, 320], P('dp'), may hold values from -6 to 6
- timesteps: int32 [64], P('dp'), may hold values from 0 to 999
- enc_in: bfloat16 [2, 320, 1280], P('pipe'), may hold values from -0.3125 to 0.3125
- enc_out: bfloat16 [2, 1280, 320], P('pipe'), may hold values from -0.15625 to 0.15625
- enc_gain: float32 [2, 320], P('pipe'), may hold values from 0.5 to 1.5
- time_gain: float32 [2, 320], P('pipe'), may hold values from -3 to 3
- dec_w: bfloat16 [2, 640, 320], P('pipe'), may hold values from -0.25 to 0.25
- dec_gain: float32 [2, 640], P('pipe'), may hold values from 0.5 to 1.5
Outputs:
- loss: float32 [], replicated
- grad_enc_in: bfloat16 [2, 320, 1280], P('pipe')
- grad_enc_out: bfloat16 [2, 1280, 320], P('pipe')
- grad_enc_gain: float32 [2, 320], P('pipe')
- grad_dec_w: bfloat16 [2, 640, 320], P('pipe')
- grad_dec_gain: float32 [2, 640], P('pipe')
All inputs are finite; a program needn't handle non-finite values.
Results may differ from a plain program's by a relative error of at most 0.004.
Values may be sent and summed in bfloat16 or wider, within the bound.
No kernel may reach another device: no remote copies, remote signals or barrier semaphores. Data moves between devices by JAX's collectives and lax.ppermute only.
A program may use at most 64 MiB of HBM per device.

v0:
```python
import math
import jax
import jax.numpy as jnp
from jax import lax
from jax.sharding import PartitionSpec as P

TSTEPS = 1000
EPS = 1e-06
GELU_SCALE = math.sqrt(2.0 / math.pi)
CUBIC = 0.044715


def from_behind(shard, axis, by):
    peers = lax.axis_size(axis)
    pairs = [(i, i + by) for i in range(peers) if 0 <= i + by < peers]
    return lax.ppermute(shard, axis, pairs)


def left_dot(matrix_a, matrix_b):
    return lax.dot_general(
        matrix_a, matrix_b, (((0,), (0,)), ((), ())), preferred_element_type=jnp.float32
    )


def right_dot(matrix_a, matrix_b):
    return lax.dot_general(
        matrix_a, matrix_b, (((1,), (1,)), ((), ())), preferred_element_type=jnp.float32
    )


def plan(step_ids):
    angles = 0.5 * math.pi * (step_ids.astype(jnp.float32) + 0.5) / TSTEPS
    return (jnp.cos(angles), jnp.sin(angles))


def features(step_ids, channels):
    half_width = channels // 2
    frequency = jnp.exp(-math.log(10000.0) * jnp.arange(half_width, dtype=jnp.float32) / half_width)
    angles = step_ids.astype(jnp.float32)[:, None] * frequency[None, :]
    return jnp.concatenate([jnp.sin(angles), jnp.cos(angles)], axis=1)


def normalize(inputs):
    values = inputs.astype(jnp.float32)
    inverse = lax.rsqrt(jnp.mean(values * values, axis=-1, keepdims=True) + EPS)
    return (values * inverse, inverse)


def norm_back(grad_unit, unit_rows, inverse):
    return (
        grad_unit - unit_rows * jnp.mean(grad_unit * unit_rows, axis=-1, keepdims=True)
    ) * inverse


def gelu_value(pre_act):
    inner = GELU_SCALE * (pre_act + CUBIC * pre_act * pre_act * pre_act)
    return 0.5 * pre_act * (1.0 + jnp.tanh(inner))


def gelu_slope(pre_act):
    tanh_val = jnp.tanh(GELU_SCALE * (pre_act + CUBIC * pre_act * pre_act * pre_act))
    return 0.5 * (1.0 + tanh_val) + 0.5 * pre_act * (1.0 - tanh_val * tanh_val) * GELU_SCALE * (
        1.0 + 3.0 * CUBIC * pre_act * pre_act
    )


def encode_parts(inputs, embedding, norm_gain, weight_in):
    unit_rows, inverse = normalize(inputs)
    normed = (unit_rows * norm_gain + embedding).astype(jnp.bfloat16)
    pre_act = jnp.dot(normed, weight_in, preferred_element_type=jnp.float32)
    hidden = gelu_value(pre_act).astype(jnp.bfloat16)
    return (unit_rows, inverse, normed, pre_act, hidden)


def encode(inputs, embedding, norm_gain, weight_in, weight_out):
    hidden = encode_parts(inputs, embedding, norm_gain, weight_in)[4]
    return (
        inputs.astype(jnp.float32) + jnp.dot(hidden, weight_out, preferred_element_type=jnp.float32)
    ).astype(jnp.bfloat16)


def encode_back(inputs, embedding, norm_gain, weight_in, weight_out, grad_y):
    unit_rows, inverse, normed, pre_act, hidden = encode_parts(
        inputs, embedding, norm_gain, weight_in
    )
    grad_out = left_dot(hidden, grad_y)
    grad_hidden = right_dot(grad_y, weight_out)
    grad_pre = (grad_hidden * gelu_slope(pre_act)).astype(jnp.bfloat16)
    grad_in = left_dot(normed, grad_pre)
    grad_normed = right_dot(grad_pre, weight_in)
    grad_gain = jnp.sum(grad_normed * unit_rows, axis=0)
    grad_x = grad_y.astype(jnp.float32) + norm_back(grad_normed * norm_gain, unit_rows, inverse)
    return (grad_x, grad_in, grad_out, grad_gain)


def decode_parts(inputs, skip_rows, norm_gain):
    channels = inputs.shape[-1]
    unit_x, inv_x = normalize(inputs)
    unit_s, inv_s = normalize(skip_rows)
    joined = jnp.concatenate(
        [unit_x * norm_gain[:channels], unit_s * norm_gain[channels:]], axis=-1
    ).astype(jnp.bfloat16)
    return (unit_x, inv_x, unit_s, inv_s, joined)


def decode(inputs, skip_rows, norm_gain, weight):
    joined = decode_parts(inputs, skip_rows, norm_gain)[4]
    return (
        inputs.astype(jnp.float32) + jnp.dot(joined, weight, preferred_element_type=jnp.float32)
    ).astype(jnp.bfloat16)


def decode_back(inputs, skip_rows, norm_gain, weight, grad_y):
    channels = inputs.shape[-1]
    unit_x, inv_x, unit_s, inv_s, joined = decode_parts(inputs, skip_rows, norm_gain)
    grad_weight = left_dot(joined, grad_y)
    grad_joined = right_dot(grad_y, weight)
    grad_gain = jnp.sum(grad_joined * jnp.concatenate([unit_x, unit_s], axis=-1), axis=0)
    scaled = grad_joined * norm_gain
    grad_x = grad_y.astype(jnp.float32) + norm_back(scaled[:, :channels], unit_x, inv_x)
    grad_skip = norm_back(scaled[:, channels:], unit_s, inv_s)
    return (grad_x, grad_skip, grad_weight, grad_gain)


def take_slot(buffer, slot_index):
    return lax.dynamic_index_in_dim(buffer, slot_index, 0, keepdims=False)


def put_slot(buffer, slot_index, value, is_valid):
    previous = take_slot(buffer, slot_index)
    return lax.dynamic_update_index_in_dim(
        buffer, jnp.where(is_valid, value, previous), slot_index, 0
    )


def body(clean, noise, timesteps, enc_in, enc_out, enc_gain, time_gain, dec_w, dec_gain):
    levels = lax.axis_size("pipe")
    section_index = lax.axis_index("pipe")
    batches, row_count, channels = clean.shape
    hidden_units = enc_in.shape[2]
    total_rows = batches * lax.axis_size("dp") * row_count
    weight_in = enc_in[0]
    weight_out = enc_out[0]
    e_gain = enc_gain[0]
    d_weight = dec_w[0]
    d_gain = dec_gain[0]
    keep_rate, spread = plan(timesteps)
    keep_full = keep_rate[:, None, None]
    spread_full = spread[:, None, None]
    clean_f = clean.astype(jnp.float32)
    noise_f = noise.astype(jnp.float32)
    start_input = (keep_full * clean_f + spread_full * noise_f).astype(jnp.bfloat16)
    target = keep_full * noise_f - spread_full * clean_f
    time_embed = time_gain[0][None, :] * features(timesteps, channels)
    is_first = section_index == 0
    is_last = section_index == levels - 1
    act_zero = jnp.zeros((row_count, channels), jnp.bfloat16)
    grad_zero = jnp.zeros((row_count, channels), jnp.float32)
    act_buffer = jnp.zeros((batches, row_count, channels), jnp.bfloat16)

    def slot_of(micro):
        is_valid = (micro >= 0) & (micro < batches)
        return (is_valid, jnp.clip(micro, 0, batches - 1))

    def forward_tick(tick, loop_state, offset, run_up, run_down):
        recv_up, recv_down, enc_keep, dec_keep, top_rows, pred_rows = loop_state
        if run_up:
            is_valid, slot_index = slot_of(tick - section_index)
            block_in = jnp.where(is_first, take_slot(start_input, slot_index), recv_up)
            embedding = take_slot(time_embed, slot_index)[None, :]
            block_out = lax.cond(
                is_valid,
                lambda: encode(block_in, embedding, e_gain, weight_in, weight_out),
                lambda: act_zero,
            )
            enc_keep = put_slot(enc_keep, slot_index, block_in, is_valid)
            top_rows = put_slot(top_rows, slot_index, block_out, is_valid & is_last)
            recv_up = from_behind(block_out, "pipe", 1)
        if run_down:
            is_valid, slot_index = slot_of(tick - offset + section_index)
            block_in = jnp.where(is_last, take_slot(top_rows, slot_index), recv_down)
            skip_rows = take_slot(enc_keep, slot_index)
            block_out = lax.cond(
                is_valid, lambda: decode(block_in, skip_rows, d_gain, d_weight), lambda: act_zero
            )
            dec_keep = put_slot(dec_keep, slot_index, block_in, is_valid)
            pred_rows = put_slot(pred_rows, slot_index, block_out, is_valid & is_first)
            recv_down = from_behind(block_out, "pipe", -1)
        return (recv_up, recv_down, enc_keep, dec_keep, top_rows, pred_rows)

    loop_state = (act_zero, act_zero, act_buffer, act_buffer, act_buffer, act_buffer)
    loop_state = lax.fori_loop(
        0,
        batches + levels - 1,
        lambda tick, state: forward_tick(tick, state, 0, True, False),
        loop_state,
    )
    loop_state = lax.fori_loop(
        0,
        batches + levels - 1,
        lambda tick, state: forward_tick(tick, state, levels - 1, False, True),
        loop_state,
    )
    enc_keep = loop_state[2]
    dec_keep = loop_state[3]
    pred_rows = loop_state[5]
    residual = pred_rows.astype(jnp.float32) - target
    local_sum = jnp.where(is_first, jnp.sum(residual * residual), jnp.float32(0.0))
    loss_value = lax.psum(local_sum, ("dp", "pipe")) / (total_rows * channels)
    grad_seed = (residual / math.sqrt(total_rows)).astype(jnp.bfloat16)

    def backward_tick(tick, loop_state, offset, run_up, run_down):
        recv_up, recv_down, skip_grads, top_grads, dec_sums, enc_sums = loop_state
        if run_up:
            is_valid, slot_index = slot_of(tick - section_index)
            grad_y = jnp.where(is_first, take_slot(grad_seed, slot_index), recv_up)
            block_x = take_slot(dec_keep, slot_index)
            skip_rows = take_slot(enc_keep, slot_index)
            grad_x, grad_skip, grad_weight, grad_gain = lax.cond(
                is_valid,
                lambda: decode_back(block_x, skip_rows, d_gain, d_weight, grad_y),
                lambda: (
                    grad_zero,
                    grad_zero,
                    jnp.zeros((2 * channels, channels), jnp.float32),
                    jnp.zeros((2 * channels,), jnp.float32),
                ),
            )
            dec_sums = (dec_sums[0] + grad_weight, dec_sums[1] + grad_gain)
            grad_sent = grad_x.astype(jnp.bfloat16)
            skip_grads = put_slot(skip_grads, slot_index, grad_skip, is_valid)
            top_grads = put_slot(top_grads, slot_index, grad_sent, is_valid & is_last)
            recv_up = from_behind(grad_sent, "pipe", 1)
        if run_down:
            is_valid, slot_index = slot_of(tick - offset + section_index)
            grad_y = jnp.where(is_last, take_slot(top_grads, slot_index), recv_down)
            block_x = take_slot(enc_keep, slot_index)
            embedding = take_slot(time_embed, slot_index)[None, :]
            grad_x, grad_in, grad_out, grad_gain = lax.cond(
                is_valid,
                lambda: encode_back(block_x, embedding, e_gain, weight_in, weight_out, grad_y),
                lambda: (
                    grad_zero,
                    jnp.zeros((channels, hidden_units), jnp.float32),
                    jnp.zeros((hidden_units, channels), jnp.float32),
                    jnp.zeros((channels,), jnp.float32),
                ),
            )
            enc_sums = (enc_sums[0] + grad_in, enc_sums[1] + grad_out, enc_sums[2] + grad_gain)
            grad_sent = (grad_x + take_slot(skip_grads, slot_index)).astype(jnp.bfloat16)
            recv_down = from_behind(grad_sent, "pipe", -1)
        return (recv_up, recv_down, skip_grads, top_grads, dec_sums, enc_sums)

    dec_start = (
        jnp.zeros((2 * channels, channels), jnp.float32),
        jnp.zeros((2 * channels,), jnp.float32),
    )
    enc_start = (
        jnp.zeros((channels, hidden_units), jnp.float32),
        jnp.zeros((hidden_units, channels), jnp.float32),
        jnp.zeros((channels,), jnp.float32),
    )
    loop_state = (
        act_zero,
        act_zero,
        jnp.zeros((batches, row_count, channels), jnp.float32),
        act_buffer,
        dec_start,
        enc_start,
    )
    dec_done = None
    loop_state = lax.fori_loop(
        0,
        batches + levels - 1,
        lambda tick, state: backward_tick(tick, state, 0, True, False),
        loop_state,
    )
    loop_state = lax.fori_loop(
        0,
        batches + levels - 1,
        lambda tick, state: backward_tick(tick, state, levels - 1, False, True),
        loop_state,
    )
    dec_sums = loop_state[4]
    enc_sums = loop_state[5]
    summed = lax.psum((enc_sums[0], enc_sums[1], enc_sums[2], dec_sums[0], dec_sums[1]), "dp")
    enc_done = (summed[0], summed[1], summed[2])
    dec_done = (summed[3], summed[4])
    return (
        loss_value,
        enc_done[0].astype(jnp.bfloat16)[None],
        enc_done[1].astype(jnp.bfloat16)[None],
        enc_done[2][None],
        dec_done[0].astype(jnp.bfloat16)[None],
        dec_done[1][None],
    )


def solution(mesh):
    in_specs = (
        P("dp", None, None),
        P("dp", None, None),
        P("dp"),
        P("pipe", None, None),
        P("pipe", None, None),
        P("pipe", None),
        P("pipe", None),
        P("pipe", None, None),
        P("pipe", None),
    )
    out_specs = (
        P(),
        P("pipe", None, None),
        P("pipe", None, None),
        P("pipe", None),
        P("pipe", None, None),
        P("pipe", None),
    )
    return jax.shard_map(body, mesh=mesh, in_specs=in_specs, out_specs=out_specs, check_vma=False)
```

profile of v0, /device:TPU:19, one launch (start us, length us, event | category | flops | bytes accessed | tf_op | source)
XLA Modules:
  0.0 368.0 jit_solution(145540141024967541)
XLA Ops:
  9.7 37.5 %while.80 = (s32[]{:T(128)}, bf16[128,320]{0,1:T(8,128)(2,1)S(1)}, bf16[4,128,320]{1,2,0:T(8,128)(2,1)S(1)}, bf16[4,128,320]{1,2,0:T(8,128)(2,1)S(1)}, s32[]{:T(...) while((s32[]{:T(128)}, bf16[128,320]{0,1:T(8,128)(2,1)S(1)}, ...), condition=%wide.region_4.5_spmd, body=%wide.region_0.4_spmd.sunk | while | flops 211763328 | bytes 3204945 | solution.py:192
  11.2 4.8 %collective-permute-done = bf16[128,320]{0,1:T(8,128)(2,1)S(1)} collective-permute-done((bf16[128,320]{0,1:T(8,128)(2,1)S(1)}, bf16[128,320]{0,1:T(8,128)(2,1)S(1)}, u32[]{:S(2)}, u32[]{:S(2)}) %collective-permute-start) | collective-permute-done | bytes 81952 | tf_op jit(solution)/shard_map/while/body/eval_jaxpr/ppermute | solution.py:16
  20.0 3.8 %collective-permute-done = bf16[128,320]{0,1:T(8,128)(2,1)S(1)} collective-permute-done((bf16[128,320]{0,1:T(8,128)(2,1)S(1)}, bf16[128,320]{0,1:T(8,128)(2,1)S(1)}, u32[]{:S(2)}, u32[]{:S(2)}) %collective-permute-start) | collective-permute-done | bytes 81952 | tf_op jit(solution)/shard_map/while/body/eval_jaxpr/ppermute | solution.py:16
  23.9 2.5 conditional.10
  27.8 3.8 %collective-permute-done = bf16[128,320]{0,1:T(8,128)(2,1)S(1)} collective-permute-done((bf16[128,320]{0,1:T(8,128)(2,1)S(1)}, bf16[128,320]{0,1:T(8,128)(2,1)S(1)}, u32[]{:S(2)}, u32[]{:S(2)}) %collective-permute-start) | collective-permute-done | bytes 81952 | tf_op jit(solution)/shard_map/while/body/eval_jaxpr/ppermute | solution.py:16
  31.7 2.5 conditional.10
  35.6 3.8 %collective-permute-done = bf16[128,320]{0,1:T(8,128)(2,1)S(1)} collective-permute-done((bf16[128,320]{0,1:T(8,128)(2,1)S(1)}, bf16[128,320]{0,1:T(8,128)(2,1)S(1)}, u32[]{:S(2)}, u32[]{:S(2)}) %collective-permute-start) | collective-permute-done | bytes 81952 | tf_op jit(solution)/shard_map/while/body/eval_jaxpr/ppermute | solution.py:16
  39.5 2.5 conditional.10
  43.4 3.8 %collective-permute-done = bf16[128,320]{0,1:T(8,128)(2,1)S(1)} collective-permute-done((bf16[128,320]{0,1:T(8,128)(2,1)S(1)}, bf16[128,320]{0,1:T(8,128)(2,1)S(1)}, u32[]{:S(2)}, u32[]{:S(2)}) %collective-permute-start) | collective-permute-done | bytes 81952 | tf_op jit(solution)/shard_map/while/body/eval_jaxpr/ppermute | solution.py:16
  47.3 29.2 %while.81 = (s32[]{:T(128)}, bf16[128,320]{0,1:T(8,128)(2,1)S(1)}, bf16[4,128,320]{1,2,0:T(8,128)(2,1)S(1)}, bf16[4,128,320]{1,2,0:T(8,128)(2,1)S(1)}, s32[]{:T(...) while((s32[]{:T(128)}, bf16[128,320]{0,1:T(8,128)(2,1)S(1)}, ...), condition=%wide.region_10.11_spmd, body=%wide.region_5.10_spmd.sunk | while | flops 53575944 | bytes 2551637 | solution.py:198
  51.8 3.7 %collective-permute-start.1 = (bf16[128,320]{0,1:T(8,128)(2,1)S(1)}, bf16[128,320]{0,1:T(8,128)(2,1)S(1)}, u32[]{:S(2)}, u32[]{:S(2)}) collective-permute-start(bf16[128,320]{0,1:T(8,128)(2,1)S(1)} %get-tuple-element.2173), channel_id=1, source_target_pairs={{1,0},{3,2},{5,4},{7,6},{9,8},{11,10},{13,12},{15,14},{17,16},{19,... | collective-permute-start | bytes 245768 | tf_op jit(solution)/shard_map/while/body/eval_jaxpr/ppermute | solution.py:16
  58.6 4.1 %collective-permute-start.1 = (bf16[128,320]{0,1:T(8,128)(2,1)S(1)}, bf16[128,320]{0,1:T(8,128)(2,1)S(1)}, u32[]{:S(2)}, u32[]{:S(2)}) collective-permute-start(bf16[128,320]{0,1:T(8,128)(2,1)S(1)} %get-tuple-element.2173), channel_id=1, source_target_pairs={{1,0},{3,2},{5,4},{7,6},{9,8},{11,10},{13,12},{15,14},{17,16},{19,... | collective-permute-start | bytes 245768 | tf_op jit(solution)/shard_map/while/body/eval_jaxpr/ppermute | solution.py:16
  65.0 4.0 %collective-permute-start.1 = (bf16[128,320]{0,1:T(8,128)(2,1)S(1)}, bf16[128,320]{0,1:T(8,128)(2,1)S(1)}, u32[]{:S(2)}, u32[]{:S(2)}) collective-permute-start(bf16[128,320]{0,1:T(8,128)(2,1)S(1)} %get-tuple-element.2173), channel_id=1, source_target_pairs={{1,0},{3,2},{5,4},{7,6},{9,8},{11,10},{13,12},{15,14},{17,16},{19,... | collective-permute-start | bytes 245768 | tf_op jit(solution)/shard_map/while/body/eval_jaxpr/ppermute | solution.py:16
  70.6 4.4 %collective-permute-start.1 = (bf16[128,320]{0,1:T(8,128)(2,1)S(1)}, bf16[128,320]{0,1:T(8,128)(2,1)S(1)}, u32[]{:S(2)}, u32[]{:S(2)}) collective-permute-start(bf16[128,320]{0,1:T(8,128)(2,1)S(1)} %get-tuple-element.2173), channel_id=1, source_target_pairs={{1,0},{3,2},{5,4},{7,6},{9,8},{11,10},{13,12},{15,14},{17,16},{19,... | collective-permute-start | bytes 245768 | tf_op jit(solution)/shard_map/while/body/eval_jaxpr/ppermute | solution.py:16
  80.4 2.7 multiply_convert_fusion.4
  83.8 51.1 %psum.42 = f32[]{:T(128)} all-reduce(f32[]{:T(128)S(6)} %select_n.216), channel_id=1, replica_groups=mesh['dp'=16,'pipe'=2] {'dp','pipe'}, use_global_device_ids=true, to_apply=%region_12.13 | all-reduce | flops 1 | bytes 8 | tf_op jit(solution)/shard_map/psum | solution.py:209
  138.1 49.6 %while.82 = (s32[]{:T(128)}, bf16[128,320]{1,0:T(8,128)(2,1)S(1)}, f32[4,128,320]{1,2,0:T(8,128)}, bf16[4,128,320]{1,2,0:T(8,128)(2,1)}, f32[640,320]{0,1:T(8,12...) while((s32[]{:T(128)}, bf16[128,320]{1,0:T(8,128)(2,1)S(1)}, ...), condition=%wide.region_21.22_spmd.clone, body=%wide.region_13.21_spmd.clone.sunk | while | flops 107316104 | bytes 10603944 | solution.py:272
  145.9 5.1 %conditional.12 = (f32[128,320]{1,0:T(8,128)S(1)}, f32[640,320]{0,1:T(8,128)S(1)}, f32[640]{0:T(1024)S(1)}, bf16[128,320]{1,0:T(8,128)(2,1)S(1)}) conditional(s32[]{:T(128)} %convert_element_type.275, () %tuple.212, (pred[]{:T(512)}, bf16[4,128,320]{2,1,0:T(8,128)(2,1)}, s32[]{:T(128)}, bf16[128,320]{1,0:T(8,128)(2,1)S(1)}, ...), branch_computations={%region_14.14_spmd, %region_15.20_spmd} | conditional | flops 106823296 | bytes 5106229 | solution.py:219
  156.4 5.1 %conditional.12 = (f32[128,320]{1,0:T(8,128)S(1)}, f32[640,320]{0,1:T(8,128)S(1)}, f32[640]{0:T(1024)S(1)}, bf16[128,320]{1,0:T(8,128)(2,1)S(1)}) conditional(s32[]{:T(128)} %convert_element_type.275, () %tuple.212, (pred[]{:T(512)}, bf16[4,128,320]{2,1,0:T(8,128)(2,1)}, s32[]{:T(128)}, bf16[128,320]{1,0:T(8,128)(2,1)S(1)}, ...), branch_computations={%region_14.14_spmd, %region_15.20_spmd} | conditional | flops 106823296 | bytes 5106229 | solution.py:219
  166.8 5.1 %conditional.12 = (f32[128,320]{1,0:T(8,128)S(1)}, f32[640,320]{0,1:T(8,128)S(1)}, f32[640]{0:T(1024)S(1)}, bf16[128,320]{1,0:T(8,128)(2,1)S(1)}) conditional(s32[]{:T(128)} %convert_element_type.275, () %tuple.212, (pred[]{:T(512)}, bf16[4,128,320]{2,1,0:T(8,128)(2,1)}, s32[]{:T(128)}, bf16[128,320]{1,0:T(8,128)(2,1)S(1)}, ...), branch_computations={%region_14.14_spmd, %region_15.20_spmd} | conditional | flops 106823296 | bytes 5106229 | solution.py:219
  177.3 5.1 %conditional.12 = (f32[128,320]{1,0:T(8,128)S(1)}, f32[640,320]{0,1:T(8,128)S(1)}, f32[640]{0:T(1024)S(1)}, bf16[128,320]{1,0:T(8,128)(2,1)S(1)}) conditional(s32[]{:T(128)} %convert_element_type.275, () %tuple.212, (pred[]{:T(512)}, bf16[4,128,320]{2,1,0:T(8,128)(2,1)}, s32[]{:T(128)}, bf16[128,320]{1,0:T(8,128)(2,1)S(1)}, ...), branch_computations={%region_14.14_spmd, %region_15.20_spmd} | conditional | flops 106823296 | bytes 5106229 | solution.py:219
  188.6 73.6 %while.83 = (s32[]{:T(128)}, bf16[128,320]{0,1:T(8,128)(2,1)S(1)}, f32[320,1280]{1,0:T(8,128)}, f32[1280,320]{0,1:T(8,128)}, f32[320]{0:T(512)S(1)}, /*index=5*/...) while((s32[]{:T(128)}, bf16[128,320]{0,1:T(8,128)(2,1)S(1)}, ...), condition=%wide.region_28.29_spmd.clone, body=%wide.region_22.28_spmd.clone.sunk | while | flops 531784128 | bytes 38364704 | solution.py:278
  188.6 7.3 %conditional.13 = (f32[128,320]{0,1:T(8,128)S(1)}, f32[320,1280]{1,0:T(8,128)S(1)}, f32[1280,320]{0,1:T(8,128)S(1)}, f32[320]{0:T(512)S(1)}) conditional(s32[]{:T(128)} %convert_element_type.277, () %tuple.215, (pred[]{:T(512)}, bf16[4,128,320]{1,2,0:T(8,128)(2,1)}, s32[]{:T(128)}, bf16[128,320]{0,1:T(8,128)(2,1)S(1)}, ...), branch_computations={%region_23.23_spmd, %region_24.27_spmd} | conditional | flops 530063168 | bytes 14685557 | solution.py:239
  202.5 7.4 %conditional.13 = (f32[128,320]{0,1:T(8,128)S(1)}, f32[320,1280]{1,0:T(8,128)S(1)}, f32[1280,320]{0,1:T(8,128)S(1)}, f32[320]{0:T(512)S(1)}) conditional(s32[]{:T(128)} %convert_element_type.277, () %tuple.215, (pred[]{:T(512)}, bf16[4,128,320]{1,2,0:T(8,128)(2,1)}, s32[]{:T(128)}, bf16[128,320]{0,1:T(8,128)(2,1)S(1)}, ...), branch_computations={%region_23.23_spmd, %region_24.27_spmd} | conditional | flops 530063168 | bytes 14685557 | solution.py:239
  213.2 2.9 select_add_fusion.12
  217.7 7.4 %conditional.13 = (f32[128,320]{0,1:T(8,128)S(1)}, f32[320,1280]{1,0:T(8,128)S(1)}, f32[1280,320]{0,1:T(8,128)S(1)}, f32[320]{0:T(512)S(1)}) conditional(s32[]{:T(128)} %convert_element_type.277, () %tuple.215, (pred[]{:T(512)}, bf16[4,128,320]{1,2,0:T(8,128)(2,1)}, s32[]{:T(128)}, bf16[128,320]{0,1:T(8,128)(2,1)S(1)}, ...), branch_computations={%region_23.23_spmd, %region_24.27_spmd} | conditional | flops 530063168 | bytes 14685557 | solution.py:239
  228.0 2.9 select_add_fusion.12
  232.6 7.4 %conditional.13 = (f32[128,320]{0,1:T(8,128)S(1)}, f32[320,1280]{1,0:T(8,128)S(1)}, f32[1280,320]{0,1:T(8,128)S(1)}, f32[320]{0:T(512)S(1)}) conditional(s32[]{:T(128)} %convert_element_type.277, () %tuple.215, (pred[]{:T(512)}, bf16[4,128,320]{1,2,0:T(8,128)(2,1)}, s32[]{:T(128)}, bf16[128,320]{0,1:T(8,128)(2,1)S(1)}, ...), branch_computations={%region_23.23_spmd, %region_24.27_spmd} | conditional | flops 530063168 | bytes 14685557 | solution.py:239
  242.8 2.9 select_add_fusion.12
  249.3 8.4 %collective-permute-start.3 = (bf16[128,320]{0,1:T(8,128)(2,1)}, bf16[128,320]{0,1:T(8,128)(2,1)S(1)}, u32[]{:S(2)}, u32[]{:S(2)}) collective-permute-start(bf16[128,320]{0,1:T(8,128)(2,1)} %fusion.110), channel_id=1, source_target_pairs={{1,0},{3,2},{5,4},{7,6},{9,8},{11,10},{13,12},{15,14},{17,16},{19,... | collective-permute-start | bytes 245768 | tf_op jit(solution)/shard_map/while/body/eval_jaxpr/ppermute | solution.py:16
  257.7 2.9 select_add_fusion.12
  262.2 104.7 %all-reduce.2 = (bf16[320,1280]{1,0:T(8,128)(2,1)}, bf16[1280,320]{0,1:T(8,128)(2,1)}, f32[1,320]{1,0:T(1,128)}, bf16[640,320]{0,1:T(8,128)(2,1)}, f32[1,640]{1,0:T(1,128)}) all-reduce(f32[320,1280]{1,0:T(8,128)} %get-tuple-element.1305, f32[1280,320]{0,1:T(8,128)} %get-tuple-element.1306, ...), channel_id=1, replica_groups=mesh['dp'=16,'pipe'=2] {'dp'}, use_global_device_ids=true, to_apply=%region_29.30 | all-reduce | flops 1024960 | bytes 6151680 | tf_op jit(solution)/shard_map/psum | solution.py:286
  (400 shorter events, 154.0 us)
Async XLA Ops:
  3.6 3.4 copy-start.10
  9.8 6.2 %collective-permute-start = (bf16[128,320]{0,1:T(8,128)(2,1)S(1)}, bf16[128,320]{0,1:T(8,128)(2,1)S(1)}, u32[]{:S(2)}, u32[]{:S(2)}) collective-permute-start(bf16[128,320]{0,1:T(8,128)(2,1)S(1)} %get-tuple-element.2172), channel_id=1, source_target_pairs={{0,1},{2,3},{4,5},{6,7},{8,9},{10,11},{12,13},{14,15},{16,17},{18,... | collective-permute-start | bytes 245768 | tf_op jit(solution)/shard_map/while/body/eval_jaxpr/ppermute | solution.py:16
  18.6 5.2 %collective-permute-start = (bf16[128,320]{0,1:T(8,128)(2,1)S(1)}, bf16[128,320]{0,1:T(8,128)(2,1)S(1)}, u32[]{:S(2)}, u32[]{:S(2)}) collective-permute-start(bf16[128,320]{0,1:T(8,128)(2,1)S(1)} %get-tuple-element.2172), channel_id=1, source_target_pairs={{0,1},{2,3},{4,5},{6,7},{8,9},{10,11},{12,13},{14,15},{16,17},{18,... | collective-permute-start | bytes 245768 | tf_op jit(solution)/shard_map/while/body/eval_jaxpr/ppermute | solution.py:16
  26.4 5.2 %collective-permute-start = (bf16[128,320]{0,1:T(8,128)(2,1)S(1)}, bf16[128,320]{0,1:T(8,128)(2,1)S(1)}, u32[]{:S(2)}, u32[]{:S(2)}) collective-permute-start(bf16[128,320]{0,1:T(8,128)(2,1)S(1)} %get-tuple-element.2172), channel_id=1, source_target_pairs={{0,1},{2,3},{4,5},{6,7},{8,9},{10,11},{12,13},{14,15},{16,17},{18,... | collective-permute-start | bytes 245768 | tf_op jit(solution)/shard_map/while/body/eval_jaxpr/ppermute | solution.py:16
  34.2 5.2 %collective-permute-start = (bf16[128,320]{0,1:T(8,128)(2,1)S(1)}, bf16[128,320]{0,1:T(8,128)(2,1)S(1)}, u32[]{:S(2)}, u32[]{:S(2)}) collective-permute-start(bf16[128,320]{0,1:T(8,128)(2,1)S(1)} %get-tuple-element.2172), channel_id=1, source_target_pairs={{0,1},{2,3},{4,5},{6,7},{8,9},{10,11},{12,13},{14,15},{16,17},{18,... | collective-permute-start | bytes 245768 | tf_op jit(solution)/shard_map/while/body/eval_jaxpr/ppermute | solution.py:16
  42.0 5.2 %collective-permute-start = (bf16[128,320]{0,1:T(8,128)(2,1)S(1)}, bf16[128,320]{0,1:T(8,128)(2,1)S(1)}, u32[]{:S(2)}, u32[]{:S(2)}) collective-permute-start(bf16[128,320]{0,1:T(8,128)(2,1)S(1)} %get-tuple-element.2172), channel_id=1, source_target_pairs={{0,1},{2,3},{4,5},{6,7},{8,9},{10,11},{12,13},{14,15},{16,17},{18,... | collective-permute-start | bytes 245768 | tf_op jit(solution)/shard_map/while/body/eval_jaxpr/ppermute | solution.py:16
  48.2 2.8 collective-permute-start.1
  51.8 5.9 %collective-permute-start.1 = (bf16[128,320]{0,1:T(8,128)(2,1)S(1)}, bf16[128,320]{0,1:T(8,128)(2,1)S(1)}, u32[]{:S(2)}, u32[]{:S(2)}) collective-permute-start(bf16[128,320]{0,1:T(8,128)(2,1)S(1)} %get-tuple-element.2173), channel_id=1, source_target_pairs={{1,0},{3,2},{5,4},{7,6},{9,8},{11,10},{13,12},{15,14},{17,16},{19,... | collective-permute-start | bytes 245768 | tf_op jit(solution)/shard_map/while/body/eval_jaxpr/ppermute | solution.py:16
  58.6 5.6 %collective-permute-start.1 = (bf16[128,320]{0,1:T(8,128)(2,1)S(1)}, bf16[128,320]{0,1:T(8,128)(2,1)S(1)}, u32[]{:S(2)}, u32[]{:S(2)}) collective-permute-start(bf16[128,320]{0,1:T(8,128)(2,1)S(1)} %get-tuple-element.2173), channel_id=1, source_target_pairs={{1,0},{3,2},{5,4},{7,6},{9,8},{11,10},{13,12},{15,14},{17,16},{19,... | collective-permute-start | bytes 245768 | tf_op jit(solution)/shard_map/while/body/eval_jaxpr/ppermute | solution.py:16
  65.0 5.5 %collective-permute-start.1 = (bf16[128,320]{0,1:T(8,128)(2,1)S(1)}, bf16[128,320]{0,1:T(8,128)(2,1)S(1)}, u32[]{:S(2)}, u32[]{:S(2)}) collective-permute-start(bf16[128,320]{0,1:T(8,128)(2,1)S(1)} %get-tuple-element.2173), channel_id=1, source_target_pairs={{1,0},{3,2},{5,4},{7,6},{9,8},{11,10},{13,12},{15,14},{17,16},{19,... | collective-permute-start | bytes 245768 | tf_op jit(solution)/shard_map/while/body/eval_jaxpr/ppermute | solution.py:16
  70.6 5.9 %collective-permute-start.1 = (bf16[128,320]{0,1:T(8,128)(2,1)S(1)}, bf16[128,320]{0,1:T(8,128)(2,1)S(1)}, u32[]{:S(2)}, u32[]{:S(2)}) collective-permute-start(bf16[128,320]{0,1:T(8,128)(2,1)S(1)} %get-tuple-element.2173), channel_id=1, source_target_pairs={{1,0},{3,2},{5,4},{7,6},{9,8},{11,10},{13,12},{15,14},{17,16},{19,... | collective-permute-start | bytes 245768 | tf_op jit(solution)/shard_map/while/body/eval_jaxpr/ppermute | solution.py:16
  76.5 59.9 %copy-start.2 = (bf16[4,128,320]{1,2,0:T(8,128)(2,1)}, bf16[4,128,320]{1,2,0:T(8,128)(2,1)S(1)}, u32[]{:S(2)}) copy-start(bf16[4,128,320]{1,2,0:T(8,128)(2,1)S(1)} %get-tuple-element.2175) | copy-start | bytes 983044
  76.5 3.9 %copy-start.6 = (bf16[4,128,320]{2,1,0:T(8,128)(2,1)S(1)}, bf16[4,128,320]{2,1,0:T(8,128)(2,1)}, u32[]{:S(2)}) copy-start(bf16[4,128,320]{2,1,0:T(8,128)(2,1)} %copy-done.5) | copy-start | bytes 983044
  80.4 57.7 %copy-start.12 = (f32[1,640]{1,0:T(1,128)S(1)}, f32[1,640]{1,0:T(1,128)}, u32[]{:S(2)}) copy-start(f32[1,640]{1,0:T(1,128)} %param.33) | copy-start | bytes 7684
  138.2 7.7 %collective-permute-start.2 = (bf16[128,320]{1,0:T(8,128)(2,1)S(1)}, bf16[128,320]{1,0:T(8,128)(2,1)S(1)}, u32[]{:S(2)}, u32[]{:S(2)}) collective-permute-start(bf16[128,320]{1,0:T(8,128)(2,1)S(1)} %get-tuple-element.1924), channel_id=1, source_target_pairs={{0,1},{2,3},{4,5},{6,7},{8,9},{10,11},{12,13},{14,15},{16,17},{18,... | collective-permute-start | bytes 245768 | tf_op jit(solution)/shard_map/while/body/eval_jaxpr/ppermute | solution.py:16
  151.0 5.4 %collective-permute-start.2 = (bf16[128,320]{1,0:T(8,128)(2,1)S(1)}, bf16[128,320]{1,0:T(8,128)(2,1)S(1)}, u32[]{:S(2)}, u32[]{:S(2)}) collective-permute-start(bf16[128,320]{1,0:T(8,128)(2,1)S(1)} %get-tuple-element.1924), channel_id=1, source_target_pairs={{0,1},{2,3},{4,5},{6,7},{8,9},{10,11},{12,13},{14,15},{16,17},{18,... | collective-permute-start | bytes 245768 | tf_op jit(solution)/shard_map/while/body/eval_jaxpr/ppermute | solution.py:16
  161.5 5.4 %collective-permute-start.2 = (bf16[128,320]{1,0:T(8,128)(2,1)S(1)}, bf16[128,320]{1,0:T(8,128)(2,1)S(1)}, u32[]{:S(2)}, u32[]{:S(2)}) collective-permute-start(bf16[128,320]{1,0:T(8,128)(2,1)S(1)} %get-tuple-element.1924), channel_id=1, source_target_pairs={{0,1},{2,3},{4,5},{6,7},{8,9},{10,11},{12,13},{14,15},{16,17},{18,... | collective-permute-start | bytes 245768 | tf_op jit(solution)/shard_map/while/body/eval_jaxpr/ppermute | solution.py:16
  171.9 5.4 %collective-permute-start.2 = (bf16[128,320]{1,0:T(8,128)(2,1)S(1)}, bf16[128,320]{1,0:T(8,128)(2,1)S(1)}, u32[]{:S(2)}, u32[]{:S(2)}) collective-permute-start(bf16[128,320]{1,0:T(8,128)(2,1)S(1)} %get-tuple-element.1924), channel_id=1, source_target_pairs={{0,1},{2,3},{4,5},{6,7},{8,9},{10,11},{12,13},{14,15},{16,17},{18,... | collective-permute-start | bytes 245768 | tf_op jit(solution)/shard_map/while/body/eval_jaxpr/ppermute | solution.py:16
  182.4 5.4 %collective-permute-start.2 = (bf16[128,320]{1,0:T(8,128)(2,1)S(1)}, bf16[128,320]{1,0:T(8,128)(2,1)S(1)}, u32[]{:S(2)}, u32[]{:S(2)}) collective-permute-start(bf16[128,320]{1,0:T(8,128)(2,1)S(1)} %get-tuple-element.1924), channel_id=1, source_target_pairs={{0,1},{2,3},{4,5},{6,7},{8,9},{10,11},{12,13},{14,15},{16,17},{18,... | collective-permute-start | bytes 245768 | tf_op jit(solution)/shard_map/while/body/eval_jaxpr/ppermute | solution.py:16
  188.6 3.7 %copy-start.9 = (bf16[1280,320]{1,0:T(8,128)(2,1)S(1)}, bf16[1280,320]{1,0:T(8,128)(2,1)}, u32[]{:S(2)}) copy-start(bf16[1280,320]{1,0:T(8,128)(2,1)} %get-tuple-element.1258) | copy-start | bytes 2457604 | tf_op jit(solution)/shard_map/while/body/eval_jaxpr/cond
  197.5 4.9 %collective-permute-start.3 = (bf16[128,320]{0,1:T(8,128)(2,1)}, bf16[128,320]{0,1:T(8,128)(2,1)S(1)}, u32[]{:S(2)}, u32[]{:S(2)}) collective-permute-start(bf16[128,320]{0,1:T(8,128)(2,1)} %fusion.110), channel_id=1, source_target_pairs={{1,0},{3,2},{5,4},{7,6},{9,8},{11,10},{13,12},{15,14},{17,16},{19,... | collective-permute-start | bytes 245768 | tf_op jit(solution)/shard_map/while/body/eval_jaxpr/ppermute | solution.py:16
  202.5 3.7 %copy-start.9 = (bf16[1280,320]{1,0:T(8,128)(2,1)S(1)}, bf16[1280,320]{1,0:T(8,128)(2,1)}, u32[]{:S(2)}) copy-start(bf16[1280,320]{1,0:T(8,128)(2,1)} %get-tuple-element.1258) | copy-start | bytes 2457604 | tf_op jit(solution)/shard_map/while/body/eval_jaxpr/cond
  211.5 6.3 %collective-permute-start.3 = (bf16[128,320]{0,1:T(8,128)(2,1)}, bf16[128,320]{0,1:T(8,128)(2,1)S(1)}, u32[]{:S(2)}, u32[]{:S(2)}) collective-permute-start(bf16[128,320]{0,1:T(8,128)(2,1)} %fusion.110), channel_id=1, source_target_pairs={{1,0},{3,2},{5,4},{7,6},{9,8},{11,10},{13,12},{15,14},{17,16},{19,... | collective-permute-start | bytes 245768 | tf_op jit(solution)/shard_map/while/body/eval_jaxpr/ppermute | solution.py:16
  213.1 3.0 copy-start
  217.8 3.7 %copy-start.9 = (bf16[1280,320]{1,0:T(8,128)(2,1)S(1)}, bf16[1280,320]{1,0:T(8,128)(2,1)}, u32[]{:S(2)}) copy-start(bf16[1280,320]{1,0:T(8,128)(2,1)} %get-tuple-element.1258) | copy-start | bytes 2457604 | tf_op jit(solution)/shard_map/while/body/eval_jaxpr/cond
  226.7 5.9 %collective-permute-start.3 = (bf16[128,320]{0,1:T(8,128)(2,1)}, bf16[128,320]{0,1:T(8,128)(2,1)S(1)}, u32[]{:S(2)}, u32[]{:S(2)}) collective-permute-start(bf16[128,320]{0,1:T(8,128)(2,1)} %fusion.110), channel_id=1, source_target_pairs={{1,0},{3,2},{5,4},{7,6},{9,8},{11,10},{13,12},{15,14},{17,16},{19,... | collective-permute-start | bytes 245768 | tf_op jit(solution)/shard_map/while/body/eval_jaxpr/ppermute | solution.py:16
  228.0 3.0 copy-start
  232.6 3.7 %copy-start.9 = (bf16[1280,320]{1,0:T(8,128)(2,1)S(1)}, bf16[1280,320]{1,0:T(8,128)(2,1)}, u32[]{:S(2)}) copy-start(bf16[1280,320]{1,0:T(8,128)(2,1)} %get-tuple-element.1258) | copy-start | bytes 2457604 | tf_op jit(solution)/shard_map/while/body/eval_jaxpr/cond
  241.5 5.9 %collective-permute-start.3 = (bf16[128,320]{0,1:T(8,128)(2,1)}, bf16[128,320]{0,1:T(8,128)(2,1)S(1)}, u32[]{:S(2)}, u32[]{:S(2)}) collective-permute-start(bf16[128,320]{0,1:T(8,128)(2,1)} %fusion.110), channel_id=1, source_target_pairs={{1,0},{3,2},{5,4},{7,6},{9,8},{11,10},{13,12},{15,14},{17,16},{19,... | collective-permute-start | bytes 245768 | tf_op jit(solution)/shard_map/while/body/eval_jaxpr/ppermute | solution.py:16
  242.8 3.0 copy-start
  249.3 12.9 %collective-permute-start.3 = (bf16[128,320]{0,1:T(8,128)(2,1)}, bf16[128,320]{0,1:T(8,128)(2,1)S(1)}, u32[]{:S(2)}, u32[]{:S(2)}) collective-permute-start(bf16[128,320]{0,1:T(8,128)(2,1)} %fusion.110), channel_id=1, source_target_pairs={{1,0},{3,2},{5,4},{7,6},{9,8},{11,10},{13,12},{15,14},{17,16},{19,... | collective-permute-start | bytes 245768 | tf_op jit(solution)/shard_map/while/body/eval_jaxpr/ppermute | solution.py:16
  257.7 3.0 copy-start
  (15 other events, 17.6 us)
where the time goes:
time: 371 us; the launch traced here: 368 us
  blocking collectives  156 us (42%)
  other arithmetic  58.6 us (16%)
  starting transfers between devices  44.4 us (12%)
  local copies, waits for them, and re-layouts  40.8 us (11%)
  matrix products  32.7 us (9%)
  waiting for transfers between devices  30.7 us (8%)
    psum x1, blocking collectives, body(): lax.psum((enc_sums[0], enc_sums[1], enc_sums[2], dec_sums[0], dec_sums[1]...  105 us
    psum x1, blocking collectives, body(): loss_value = lax.psum(local_sum, ('dp', 'pipe')) / (total_rows * channels)  51.1 us
    ppermute x20, starting transfers between devices, from_behind(): return lax.ppermute(shard, axis, pairs)  44.4 us
    ppermute x20, waiting for transfers between devices, from_behind(): return lax.ppermute(shard, axis, pairs)  30.7 us
    add x5, other arithmetic, backward_tick(): enc_sums[0] + grad_in  13.1 us
    dynamic_slice x48, local copies, waits for them, and re-layouts, take_slot(): return lax.dynamic_index_in_dim(buffer, slot_index, 0, keepdims=False)  10.9 us
    dot_general x12, matrix products, right_dot(): lax.dot_general(matrix_a, matrix_b, (((1,), (1,)), ((), ())), preferred_e...  9.99 us
    dot_general x4, matrix products, encode(): jnp.dot(hidden, weight_out, preferred_element_type=jnp.float32)  9.62 us
  transfers between devices with their start and end apart: 20, of which 15 were waited for; matrix products, arithmetic and copies ran while one was open for 10% of the time, Pallas kernels for 0%

commit v1 on v0

--- a/solution.py
+++ b/solution.py
@@ -206,7 +206,12 @@
     pred_rows = loop_state[5]
     residual = pred_rows.astype(jnp.float32) - target
     local_sum = jnp.where(is_first, jnp.sum(residual * residual), jnp.float32(0.0))
-    loss_value = lax.psum(local_sum, ("dp", "pipe")) / (total_rows * channels)
+
+    def domain_fill(work_x):
+        left_arr = jax.lax.all_gather(work_x, axis_name=("dp", "pipe"))
+        return jnp.sum(left_arr, 0)
+
+    loss_value = domain_fill(local_sum) / (total_rows * channels)
     grad_seed = (residual / math.sqrt(total_rows)).astype(jnp.bfloat16)
 
     def backward_tick(tick, loop_state, offset, run_up, run_down):

time: 371 us -> 358 us (0.965)
  local copies, waits for them, and re-layouts: 40.8 us -> 27.4 us
  other arithmetic: 58.6 us -> 62.4 us
    psum x1 -> x0, blocking collectives: 51.1 us -> none  [body(): loss_value = lax.psum(local_sum, ('dp', 'pipe')) / (total_rows * channels)]
    unnamed x0 -> x1, blocking collectives: none -> 50.8 us
    add x5, other arithmetic: 2.12 us -> 12.7 us  [backward_tick(): enc_sums[1] + grad_out]
    add x10, other arithmetic: 1.07 us -> 9.5 us  [backward_tick(): dec_sums = (dec_sums[0] + grad_weight, dec_sums[1] + grad_gain)]
    select_n x4, other arithmetic: 3.94 us -> 0.04 us  [backward_tick(): grad_y = jnp.where(is_last, take_slot(top_grads, slot_index), recv_down)]
    unnamed x24 -> x26, local copies, waits for them, and re-layouts: 9.24 us -> 5.95 us
  transfers between devices with their start and end apart: 20 -> 20, of which waited for: 15 -> 11; matrix products, arithmetic and copies ran while one was open for 10% -> 13% of each run, Pallas kernels for 0% -> 0%
where the time goes in v1:
time: 358 us; the launch traced here: 355 us
  blocking collectives  153 us (43%)
  other arithmetic  62.4 us (17%)
  starting transfers between devices  45.1 us (13%)
  matrix products  32.7 us (9%)
  waiting for transfers between devices  28.6 us (8%)
  local copies, waits for them, and re-layouts  27.4 us (8%)
    psum x1, blocking collectives, body(): lax.psum((enc_sums[0], enc_sums[1], enc_sums[2], dec_sums[0], dec_sums[1]...  102 us
    unnamed x1, blocking collectives  50.8 us
    ppermute x20, starting transfers between devices, from_behind(): return lax.ppermute(shard, axis, pairs)  45.1 us
    ppermute x20, waiting for transfers between devices, from_behind(): return lax.ppermute(shard, axis, pairs)  28.6 us
    add x5, other arithmetic, backward_tick(): enc_sums[1] + grad_out  12.7 us
    add x5, other arithmetic, backward_tick(): enc_sums[0] + grad_in  12.7 us
    dot_general x12, matrix products, right_dot(): lax.dot_general(matrix_a, matrix_b, (((1,), (1,)), ((), ())), preferred_e...  9.98 us
    dot_general x4, matrix products, encode(): jnp.dot(hidden, weight_out, preferred_element_type=jnp.float32)  9.62 us
  transfers between devices with their start and end apart: 20, of which 11 were waited for; matrix products, arithmetic and copies ran while one was open for 13% of the time, Pallas kernels for 0%

profile of v1, /device:TPU:19, one launch (start us, length us, event | category | flops | bytes accessed | tf_op | source)
XLA Modules:
  0.0 354.5 jit_solution(12865316952814536737)
XLA Ops:
  9.2 37.5 %while.80 = (s32[]{:T(128)}, bf16[128,320]{0,1:T(8,128)(2,1)S(1)}, bf16[4,128,320]{1,2,0:T(8,128)(2,1)S(1)}, bf16[4,128,320]{1,2,0:T(8,128)(2,1)S(1)}, s32[]{:T(...) while((s32[]{:T(128)}, bf16[128,320]{0,1:T(8,128)(2,1)S(1)}, ...), condition=%wide.region_4.5_spmd, body=%wide.region_0.4_spmd.sunk | while | flops 211763328 | bytes 3204945 | solution.py:192
  10.7 4.8 %collective-permute-done = bf16[128,320]{0,1:T(8,128)(2,1)S(1)} collective-permute-done((bf16[128,320]{0,1:T(8,128)(2,1)S(1)}, bf16[128,320]{0,1:T(8,128)(2,1)S(1)}, u32[]{:S(2)}, u32[]{:S(2)}) %collective-permute-start) | collective-permute-done | bytes 81952 | tf_op jit(solution)/shard_map/while/body/eval_jaxpr/ppermute | solution.py:16
  15.6 2.5 conditional.10
  19.5 3.8 %collective-permute-done = bf16[128,320]{0,1:T(8,128)(2,1)S(1)} collective-permute-done((bf16[128,320]{0,1:T(8,128)(2,1)S(1)}, bf16[128,320]{0,1:T(8,128)(2,1)S(1)}, u32[]{:S(2)}, u32[]{:S(2)}) %collective-permute-start) | collective-permute-done | bytes 81952 | tf_op jit(solution)/shard_map/while/body/eval_jaxpr/ppermute | solution.py:16
  23.4 2.5 conditional.10
  27.3 3.8 %collective-permute-done = bf16[128,320]{0,1:T(8,128)(2,1)S(1)} collective-permute-done((bf16[128,320]{0,1:T(8,128)(2,1)S(1)}, bf16[128,320]{0,1:T(8,128)(2,1)S(1)}, u32[]{:S(2)}, u32[]{:S(2)}) %collective-permute-start) | collective-permute-done | bytes 81952 | tf_op jit(solution)/shard_map/while/body/eval_jaxpr/ppermute | solution.py:16
  35.1 3.8 %collective-permute-done = bf16[128,320]{0,1:T(8,128)(2,1)S(1)} collective-permute-done((bf16[128,320]{0,1:T(8,128)(2,1)S(1)}, bf16[128,320]{0,1:T(8,128)(2,1)S(1)}, u32[]{:S(2)}, u32[]{:S(2)}) %collective-permute-start) | collective-permute-done | bytes 81952 | tf_op jit(solution)/shard_map/while/body/eval_jaxpr/ppermute | solution.py:16
  39.0 2.5 conditional.10
  42.9 3.8 %collective-permute-done = bf16[128,320]{0,1:T(8,128)(2,1)S(1)} collective-permute-done((bf16[128,320]{0,1:T(8,128)(2,1)S(1)}, bf16[128,320]{0,1:T(8,128)(2,1)S(1)}, u32[]{:S(2)}, u32[]{:S(2)}) %collective-permute-start) | collective-permute-done | bytes 81952 | tf_op jit(solution)/shard_map/while/body/eval_jaxpr/ppermute | solution.py:16
  47.3 29.1 %while.81 = (s32[]{:T(128)}, bf16[128,320]{0,1:T(8,128)(2,1)S(1)}, bf16[4,128,320]{1,2,0:T(8,128)(2,1)S(1)}, bf16[4,128,320]{1,2,0:T(8,128)(2,1)S(1)}, s32[]{:T(...) while((s32[]{:T(128)}, bf16[128,320]{0,1:T(8,128)(2,1)S(1)}, ...), condition=%wide.region_10.11_spmd, body=%wide.region_5.10_spmd.sunk | while | flops 53575944 | bytes 2551637 | solution.py:198
  51.8 3.7 %collective-permute-start.1 = (bf16[128,320]{0,1:T(8,128)(2,1)S(1)}, bf16[128,320]{0,1:T(8,128)(2,1)S(1)}, u32[]{:S(2)}, u32[]{:S(2)}) collective-permute-start(bf16[128,320]{0,1:T(8,128)(2,1)S(1)} %get-tuple-element.2173), channel_id=1, source_target_pairs={{1,0},{3,2},{5,4},{7,6},{9,8},{11,10},{13,12},{15,14},{17,16},{19,... | collective-permute-start | bytes 245768 | tf_op jit(solution)/shard_map/while/body/eval_jaxpr/ppermute | solution.py:16
  58.5 4.1 %collective-permute-start.1 = (bf16[128,320]{0,1:T(8,128)(2,1)S(1)}, bf16[128,320]{0,1:T(8,128)(2,1)S(1)}, u32[]{:S(2)}, u32[]{:S(2)}) collective-permute-start(bf16[128,320]{0,1:T(8,128)(2,1)S(1)} %get-tuple-element.2173), channel_id=1, source_target_pairs={{1,0},{3,2},{5,4},{7,6},{9,8},{11,10},{13,12},{15,14},{17,16},{19,... | collective-permute-start | bytes 245768 | tf_op jit(solution)/shard_map/while/body/eval_jaxpr/ppermute | solution.py:16
  64.9 4.0 %collective-permute-start.1 = (bf16[128,320]{0,1:T(8,128)(2,1)S(1)}, bf16[128,320]{0,1:T(8,128)(2,1)S(1)}, u32[]{:S(2)}, u32[]{:S(2)}) collective-permute-start(bf16[128,320]{0,1:T(8,128)(2,1)S(1)} %get-tuple-element.2173), channel_id=1, source_target_pairs={{1,0},{3,2},{5,4},{7,6},{9,8},{11,10},{13,12},{15,14},{17,16},{19,... | collective-permute-start | bytes 245768 | tf_op jit(solution)/shard_map/while/body/eval_jaxpr/ppermute | solution.py:16
  70.5 4.4 %collective-permute-start.1 = (bf16[128,320]{0,1:T(8,128)(2,1)S(1)}, bf16[128,320]{0,1:T(8,128)(2,1)S(1)}, u32[]{:S(2)}, u32[]{:S(2)}) collective-permute-start(bf16[128,320]{0,1:T(8,128)(2,1)S(1)} %get-tuple-element.2173), channel_id=1, source_target_pairs={{1,0},{3,2},{5,4},{7,6},{9,8},{11,10},{13,12},{15,14},{17,16},{19,... | collective-permute-start | bytes 245768 | tf_op jit(solution)/shard_map/while/body/eval_jaxpr/ppermute | solution.py:16
  79.4 50.8 %all-reduce = f32[32]{0:T(128)S(1)} all-reduce(f32[32]{0:T(128)S(1)} %dynamic-update-slice), channel_id=1, replica_groups=mesh['dp'=16,'pipe'=2] {'dp','pipe'}, use_global_device_ids=true, to_apply=%add | all-reduce | flops 32 | bytes 256
  132.7 37.9 %while.82 = (s32[]{:T(128)}, bf16[128,320]{1,0:T(8,128)(2,1)S(1)}, f32[4,128,320]{1,2,0:T(8,128)}, bf16[4,128,320]{1,2,0:T(8,128)(2,1)S(1)}, f32[640,320]{0,1:T(...) while((s32[]{:T(128)}, bf16[128,320]{1,0:T(8,128)(2,1)S(1)}, ...), condition=%wide.region_21.22_spmd.clone, body=%wide.region_13.21_spmd.clone.sunk | while | flops 107316104 | bytes 10603436 | solution.py:277
  170.6 80.6 %while.83 = (s32[]{:T(128)}, bf16[128,320]{0,1:T(8,128)(2,1)S(1)}, f32[320,1280]{1,0:T(8,128)}, f32[1280,320]{0,1:T(8,128)}, f32[320]{0:T(512)S(1)}, /*index=5*/...) while((s32[]{:T(128)}, bf16[128,320]{0,1:T(8,128)(2,1)S(1)}, ...), condition=%wide.region_28.29_spmd.clone, body=%wide.region_22.28_spmd.clone.sunk | while | flops 531784128 | bytes 27878944 | solution.py:283
  171.4 7.1 %conditional.13 = (f32[128,320]{0,1:T(8,128)S(1)}, f32[320,1280]{1,0:T(8,128)S(1)}, f32[1280,320]{0,1:T(8,128)S(1)}, f32[320]{0:T(512)S(1)}) conditional(s32[]{:T(128)} %convert_element_type.277, () %tuple.215, (pred[]{:T(512)}, bf16[4,128,320]{1,2,0:T(8,128)(2,1)S(1)}, s32[]{:T(128)}, bf16[128,320]{0,1:T(8,128)(2,1)S(1)}, ...), branch_computations={%region_23.23_spmd, %region_24.27_spmd} | conditional | flops 530063168 | bytes 14685557 | solution.py:244
  184.9 7.1 %conditional.13 = (f32[128,320]{0,1:T(8,128)S(1)}, f32[320,1280]{1,0:T(8,128)S(1)}, f32[1280,320]{0,1:T(8,128)S(1)}, f32[320]{0:T(512)S(1)}) conditional(s32[]{:T(128)} %convert_element_type.277, () %tuple.215, (pred[]{:T(512)}, bf16[4,128,320]{1,2,0:T(8,128)(2,1)S(1)}, s32[]{:T(128)}, bf16[128,320]{0,1:T(8,128)(2,1)S(1)}, ...), branch_computations={%region_23.23_spmd, %region_24.27_spmd} | conditional | flops 530063168 | bytes 14685557 | solution.py:244
  193.6 2.6 collective-permute-start.3
  196.2 2.8 select_add_fusion.12
  199.0 2.8 select_add_fusion.13
  202.6 7.1 %conditional.13 = (f32[128,320]{0,1:T(8,128)S(1)}, f32[320,1280]{1,0:T(8,128)S(1)}, f32[1280,320]{0,1:T(8,128)S(1)}, f32[320]{0:T(512)S(1)}) conditional(s32[]{:T(128)} %convert_element_type.277, () %tuple.215, (pred[]{:T(512)}, bf16[4,128,320]{1,2,0:T(8,128)(2,1)S(1)}, s32[]{:T(128)}, bf16[128,320]{0,1:T(8,128)(2,1)S(1)}, ...), branch_computations={%region_23.23_spmd, %region_24.27_spmd} | conditional | flops 530063168 | bytes 14685557 | solution.py:244
  212.7 2.8 select_add_fusion.12
  215.5 2.8 select_add_fusion.13
  219.1 7.1 %conditional.13 = (f32[128,320]{0,1:T(8,128)S(1)}, f32[320,1280]{1,0:T(8,128)S(1)}, f32[1280,320]{0,1:T(8,128)S(1)}, f32[320]{0:T(512)S(1)}) conditional(s32[]{:T(128)} %convert_element_type.277, () %tuple.215, (pred[]{:T(512)}, bf16[4,128,320]{1,2,0:T(8,128)(2,1)S(1)}, s32[]{:T(128)}, bf16[128,320]{0,1:T(8,128)(2,1)S(1)}, ...), branch_computations={%region_23.23_spmd, %region_24.27_spmd} | conditional | flops 530063168 | bytes 14685557 | solution.py:244
  229.1 2.8 select_add_fusion.12
  231.9 2.8 select_add_fusion.13
  237.4 8.2 %collective-permute-start.3 = (bf16[128,320]{0,1:T(8,128)(2,1)}, bf16[128,320]{0,1:T(8,128)(2,1)S(1)}, u32[]{:S(2)}, u32[]{:S(2)}) collective-permute-start(bf16[128,320]{0,1:T(8,128)(2,1)} %fusion.110), channel_id=1, source_target_pairs={{1,0},{3,2},{5,4},{7,6},{9,8},{11,10},{13,12},{15,14},{17,16},{19,... | collective-permute-start | bytes 245768 | tf_op jit(solution)/shard_map/while/body/eval_jaxpr/ppermute | solution.py:16
  245.5 2.8 select_add_fusion.12
  248.4 2.8 select_add_fusion.13
  251.2 102.2 %all-reduce.3 = (bf16[320,1280]{1,0:T(8,128)(2,1)}, bf16[1280,320]{0,1:T(8,128)(2,1)}, f32[1,320]{1,0:T(1,128)}, bf16[640,320]{0,1:T(8,128)(2,1)}, f32[1,640]{1,0:T(1,128)}) all-reduce(f32[320,1280]{1,0:T(8,128)} %get-tuple-element.1305, f32[1280,320]{0,1:T(8,128)} %get-tuple-element.1306, ...), channel_id=1, replica_groups=mesh['dp'=16,'pipe'=2] {'dp'}, use_global_device_ids=true, to_apply=%region_29.30 | all-reduce | flops 1024960 | bytes 6151680 | tf_op jit(solution)/shard_map/psum | solution.py:291
  (403 shorter events, 142.2 us)
Async XLA Ops:
  2.0 4.1 %copy-start.9 = (f32[4]{0:T(128)}, f32[4]{0:T(128)S(1)}, u32[]{:S(2)}) copy-start(f32[4]{0:T(128)S(1)} %get-tuple-element.1604) | copy-start | bytes 52
  2.0 4.1 %copy-start.11 = (f32[4]{0:T(128)}, f32[4]{0:T(128)S(1)}, u32[]{:S(2)}) copy-start(f32[4]{0:T(128)S(1)} %get-tuple-element.1605) | copy-start | bytes 52
  3.7 2.9 copy-start.5
  9.4 6.2 %collective-permute-start = (bf16[128,320]{0,1:T(8,128)(2,1)S(1)}, bf16[128,320]{0,1:T(8,128)(2,1)S(1)}, u32[]{:S(2)}, u32[]{:S(2)}) collective-permute-start(bf16[128,320]{0,1:T(8,128)(2,1)S(1)} %get-tuple-element.2172), channel_id=1, source_target_pairs={{0,1},{2,3},{4,5},{6,7},{8,9},{10,11},{12,13},{14,15},{16,17},{18,... | collective-permute-start | bytes 245768 | tf_op jit(solution)/shard_map/while/body/eval_jaxpr/ppermute | solution.py:16
  18.1 5.2 %collective-permute-start = (bf16[128,320]{0,1:T(8,128)(2,1)S(1)}, bf16[128,320]{0,1:T(8,128)(2,1)S(1)}, u32[]{:S(2)}, u32[]{:S(2)}) collective-permute-start(bf16[128,320]{0,1:T(8,128)(2,1)S(1)} %get-tuple-element.2172), channel_id=1, source_target_pairs={{0,1},{2,3},{4,5},{6,7},{8,9},{10,11},{12,13},{14,15},{16,17},{18,... | collective-permute-start | bytes 245768 | tf_op jit(solution)/shard_map/while/body/eval_jaxpr/ppermute | solution.py:16
  25.9 5.2 %collective-permute-start = (bf16[128,320]{0,1:T(8,128)(2,1)S(1)}, bf16[128,320]{0,1:T(8,128)(2,1)S(1)}, u32[]{:S(2)}, u32[]{:S(2)}) collective-permute-start(bf16[128,320]{0,1:T(8,128)(2,1)S(1)} %get-tuple-element.2172), channel_id=1, source_target_pairs={{0,1},{2,3},{4,5},{6,7},{8,9},{10,11},{12,13},{14,15},{16,17},{18,... | collective-permute-start | bytes 245768 | tf_op jit(solution)/shard_map/while/body/eval_jaxpr/ppermute | solution.py:16
  33.7 5.2 %collective-permute-start = (bf16[128,320]{0,1:T(8,128)(2,1)S(1)}, bf16[128,320]{0,1:T(8,128)(2,1)S(1)}, u32[]{:S(2)}, u32[]{:S(2)}) collective-permute-start(bf16[128,320]{0,1:T(8,128)(2,1)S(1)} %get-tuple-element.2172), channel_id=1, source_target_pairs={{0,1},{2,3},{4,5},{6,7},{8,9},{10,11},{12,13},{14,15},{16,17},{18,... | collective-permute-start | bytes 245768 | tf_op jit(solution)/shard_map/while/body/eval_jaxpr/ppermute | solution.py:16
  41.5 5.2 %collective-permute-start = (bf16[128,320]{0,1:T(8,128)(2,1)S(1)}, bf16[128,320]{0,1:T(8,128)(2,1)S(1)}, u32[]{:S(2)}, u32[]{:S(2)}) collective-permute-start(bf16[128,320]{0,1:T(8,128)(2,1)S(1)} %get-tuple-element.2172), channel_id=1, source_target_pairs={{0,1},{2,3},{4,5},{6,7},{8,9},{10,11},{12,13},{14,15},{16,17},{18,... | collective-permute-start | bytes 245768 | tf_op jit(solution)/shard_map/while/body/eval_jaxpr/ppermute | solution.py:16
  46.9 30.0 %copy-start.10 = (f32[4]{0:T(128)S(1)}, f32[4]{0:T(128)}, u32[]{:S(2)}) copy-start(f32[4]{0:T(128)} %copy-done.9) | copy-start | bytes 52
  46.9 30.0 %copy-start.12 = (f32[4]{0:T(128)S(1)}, f32[4]{0:T(128)}, u32[]{:S(2)}) copy-start(f32[4]{0:T(128)} %copy-done.11) | copy-start | bytes 52
  48.2 2.8 collective-permute-start.1
  51.8 5.9 %collective-permute-start.1 = (bf16[128,320]{0,1:T(8,128)(2,1)S(1)}, bf16[128,320]{0,1:T(8,128)(2,1)S(1)}, u32[]{:S(2)}, u32[]{:S(2)}) collective-permute-start(bf16[128,320]{0,1:T(8,128)(2,1)S(1)} %get-tuple-element.2173), channel_id=1, source_target_pairs={{1,0},{3,2},{5,4},{7,6},{9,8},{11,10},{13,12},{15,14},{17,16},{19,... | collective-permute-start | bytes 245768 | tf_op jit(solution)/shard_map/while/body/eval_jaxpr/ppermute | solution.py:16
  58.5 5.6 %collective-permute-start.1 = (bf16[128,320]{0,1:T(8,128)(2,1)S(1)}, bf16[128,320]{0,1:T(8,128)(2,1)S(1)}, u32[]{:S(2)}, u32[]{:S(2)}) collective-permute-start(bf16[128,320]{0,1:T(8,128)(2,1)S(1)} %get-tuple-element.2173), channel_id=1, source_target_pairs={{1,0},{3,2},{5,4},{7,6},{9,8},{11,10},{13,12},{15,14},{17,16},{19,... | collective-permute-start | bytes 245768 | tf_op jit(solution)/shard_map/while/body/eval_jaxpr/ppermute | solution.py:16
  64.9 5.5 %collective-permute-start.1 = (bf16[128,320]{0,1:T(8,128)(2,1)S(1)}, bf16[128,320]{0,1:T(8,128)(2,1)S(1)}, u32[]{:S(2)}, u32[]{:S(2)}) collective-permute-start(bf16[128,320]{0,1:T(8,128)(2,1)S(1)} %get-tuple-element.2173), channel_id=1, source_target_pairs={{1,0},{3,2},{5,4},{7,6},{9,8},{11,10},{13,12},{15,14},{17,16},{19,... | collective-permute-start | bytes 245768 | tf_op jit(solution)/shard_map/while/body/eval_jaxpr/ppermute | solution.py:16
  70.5 5.9 %collective-permute-start.1 = (bf16[128,320]{0,1:T(8,128)(2,1)S(1)}, bf16[128,320]{0,1:T(8,128)(2,1)S(1)}, u32[]{:S(2)}, u32[]{:S(2)}) collective-permute-start(bf16[128,320]{0,1:T(8,128)(2,1)S(1)} %get-tuple-element.2173), channel_id=1, source_target_pairs={{1,0},{3,2},{5,4},{7,6},{9,8},{11,10},{13,12},{15,14},{17,16},{19,... | collective-permute-start | bytes 245768 | tf_op jit(solution)/shard_map/while/body/eval_jaxpr/ppermute | solution.py:16
  76.4 56.2 %copy-start = (bf16[4,128,320]{1,2,0:T(8,128)(2,1)}, bf16[4,128,320]{1,2,0:T(8,128)(2,1)S(1)}, u32[]{:S(2)}) copy-start(bf16[4,128,320]{1,2,0:T(8,128)(2,1)S(1)} %get-tuple-element.2175) | copy-start | bytes 983044
  76.9 55.8 %copy-start.7 = (f32[1,640]{1,0:T(1,128)S(1)}, f32[1,640]{1,0:T(1,128)}, u32[]{:S(2)}) copy-start(f32[1,640]{1,0:T(1,128)} %param.33) | copy-start | bytes 7684
  132.8 5.4 %collective-permute-start.2 = (bf16[128,320]{1,0:T(8,128)(2,1)S(1)}, bf16[128,320]{1,0:T(8,128)(2,1)S(1)}, u32[]{:S(2)}, u32[]{:S(2)}) collective-permute-start(bf16[128,320]{1,0:T(8,128)(2,1)S(1)} %get-tuple-element.1924), channel_id=1, source_target_pairs={{0,1},{2,3},{4,5},{6,7},{8,9},{10,11},{12,13},{14,15},{16,17},{18,... | collective-permute-start | bytes 245768 | tf_op jit(solution)/shard_map/while/body/eval_jaxpr/ppermute | solution.py:16
  140.6 5.7 %collective-permute-start.2 = (bf16[128,320]{1,0:T(8,128)(2,1)S(1)}, bf16[128,320]{1,0:T(8,128)(2,1)S(1)}, u32[]{:S(2)}, u32[]{:S(2)}) collective-permute-start(bf16[128,320]{1,0:T(8,128)(2,1)S(1)} %get-tuple-element.1924), channel_id=1, source_target_pairs={{0,1},{2,3},{4,5},{6,7},{8,9},{10,11},{12,13},{14,15},{16,17},{18,... | collective-permute-start | bytes 245768 | tf_op jit(solution)/shard_map/while/body/eval_jaxpr/ppermute | solution.py:16
  148.7 5.7 %collective-permute-start.2 = (bf16[128,320]{1,0:T(8,128)(2,1)S(1)}, bf16[128,320]{1,0:T(8,128)(2,1)S(1)}, u32[]{:S(2)}, u32[]{:S(2)}) collective-permute-start(bf16[128,320]{1,0:T(8,128)(2,1)S(1)} %get-tuple-element.1924), channel_id=1, source_target_pairs={{0,1},{2,3},{4,5},{6,7},{8,9},{10,11},{12,13},{14,15},{16,17},{18,... | collective-permute-start | bytes 245768 | tf_op jit(solution)/shard_map/while/body/eval_jaxpr/ppermute | solution.py:16
  156.8 5.7 %collective-permute-start.2 = (bf16[128,320]{1,0:T(8,128)(2,1)S(1)}, bf16[128,320]{1,0:T(8,128)(2,1)S(1)}, u32[]{:S(2)}, u32[]{:S(2)}) collective-permute-start(bf16[128,320]{1,0:T(8,128)(2,1)S(1)} %get-tuple-element.1924), channel_id=1, source_target_pairs={{0,1},{2,3},{4,5},{6,7},{8,9},{10,11},{12,13},{14,15},{16,17},{18,... | collective-permute-start | bytes 245768 | tf_op jit(solution)/shard_map/while/body/eval_jaxpr/ppermute | solution.py:16
  164.9 5.7 %collective-permute-start.2 = (bf16[128,320]{1,0:T(8,128)(2,1)S(1)}, bf16[128,320]{1,0:T(8,128)(2,1)S(1)}, u32[]{:S(2)}, u32[]{:S(2)}) collective-permute-start(bf16[128,320]{1,0:T(8,128)(2,1)S(1)} %get-tuple-element.1924), channel_id=1, source_target_pairs={{0,1},{2,3},{4,5},{6,7},{8,9},{10,11},{12,13},{14,15},{16,17},{18,... | collective-permute-start | bytes 245768 | tf_op jit(solution)/shard_map/while/body/eval_jaxpr/ppermute | solution.py:16
  171.4 3.5 copy-start.4
  180.1 4.1 %collective-permute-start.3 = (bf16[128,320]{0,1:T(8,128)(2,1)}, bf16[128,320]{0,1:T(8,128)(2,1)S(1)}, u32[]{:S(2)}, u32[]{:S(2)}) collective-permute-start(bf16[128,320]{0,1:T(8,128)(2,1)} %fusion.110), channel_id=1, source_target_pairs={{1,0},{3,2},{5,4},{7,6},{9,8},{11,10},{13,12},{15,14},{17,16},{19,... | collective-permute-start | bytes 245768 | tf_op jit(solution)/shard_map/while/body/eval_jaxpr/ppermute | solution.py:16
  184.9 3.5 copy-start.4
  193.6 8.3 %collective-permute-start.3 = (bf16[128,320]{0,1:T(8,128)(2,1)}, bf16[128,320]{0,1:T(8,128)(2,1)S(1)}, u32[]{:S(2)}, u32[]{:S(2)}) collective-permute-start(bf16[128,320]{0,1:T(8,128)(2,1)} %fusion.110), channel_id=1, source_target_pairs={{1,0},{3,2},{5,4},{7,6},{9,8},{11,10},{13,12},{15,14},{17,16},{19,... | collective-permute-start | bytes 245768 | tf_op jit(solution)/shard_map/while/body/eval_jaxpr/ppermute | solution.py:16
  199.0 2.9 copy-start.3
  202.6 3.5 copy-start.4
  211.4 7.0 %collective-permute-start.3 = (bf16[128,320]{0,1:T(8,128)(2,1)}, bf16[128,320]{0,1:T(8,128)(2,1)S(1)}, u32[]{:S(2)}, u32[]{:S(2)}) collective-permute-start(bf16[128,320]{0,1:T(8,128)(2,1)} %fusion.110), channel_id=1, source_target_pairs={{1,0},{3,2},{5,4},{7,6},{9,8},{11,10},{13,12},{15,14},{17,16},{19,... | collective-permute-start | bytes 245768 | tf_op jit(solution)/shard_map/while/body/eval_jaxpr/ppermute | solution.py:16
  219.1 3.5 copy-start.4
  227.8 7.0 %collective-permute-start.3 = (bf16[128,320]{0,1:T(8,128)(2,1)}, bf16[128,320]{0,1:T(8,128)(2,1)S(1)}, u32[]{:S(2)}, u32[]{:S(2)}) collective-permute-start(bf16[128,320]{0,1:T(8,128)(2,1)} %fusion.110), channel_id=1, source_target_pairs={{1,0},{3,2},{5,4},{7,6},{9,8},{11,10},{13,12},{15,14},{17,16},{19,... | collective-permute-start | bytes 245768 | tf_op jit(solution)/shard_map/while/body/eval_jaxpr/ppermute | solution.py:16
  237.4 13.9 %collective-permute-start.3 = (bf16[128,320]{0,1:T(8,128)(2,1)}, bf16[128,320]{0,1:T(8,128)(2,1)S(1)}, u32[]{:S(2)}, u32[]{:S(2)}) collective-permute-start(bf16[128,320]{0,1:T(8,128)(2,1)} %fusion.110), channel_id=1, source_target_pairs={{1,0},{3,2},{5,4},{7,6},{9,8},{11,10},{13,12},{15,14},{17,16},{19,... | collective-permute-start | bytes 245768 | tf_op jit(solution)/shard_map/while/body/eval_jaxpr/ppermute | solution.py:16
  (15 other events, 20.7 us)
